TPU v7x, 512 devices: a whole 4x8x8 slice. The times are simulated.
512 devices in a mesh: pair: 32 (over y, x), row: 16 (over z, core).
Axes of the slice: x: 4, y: 8, z: 8, core: 2. Of those that a mesh axis runs over, the one named last changes fastest.
Arguments:
- r_factor: float32 [16384, 16384], P(('row', 'pair')), may hold values from -40 to 40, as said below
- block_slots: int32 [256], replicated, may hold values from 0 to 255, as said below
Outputs:
- rotated: float32 [16384, 16384], P('row', 'pair')
- off_ratio: float32 [], replicated
Inputs may be any that keep to these rules, and one draw needn't show every extreme that they name: `block_slots`: each of the 256 column blocks appears exactly once. `r_factor`: entries below the diagonal are zero and the diagonal is positive.
All inputs are finite; a program needn't handle non-finite values.
Results may differ from a plain program's by a relative error of at most 0.0001.
Values sent between devices are 32-bit elements; how exact they have to be, the bound alone decides.
A program may use at most 64 MiB of HBM per device.

v0:
```python
import jax
import jax.numpy as jnp
from jax import lax
from jax.sharding import PartitionSpec as P

BLOCK = 64
ITERS = 3


def passed_along(value, axis, by):
    count = lax.axis_size(axis)
    pairs = [(i, i + by) for i in range(count) if 0 <= i + by < count]
    return lax.ppermute(value, axis, pairs)


def cayley(pair_gram):
    size_n = pair_gram.shape[0]
    diag_vals = jnp.diagonal(pair_gram)
    spread = diag_vals[:, None] - diag_vals[None, :]
    denom = 2.0 * (diag_vals[:, None] ** 2 + diag_vals[None, :] ** 2)
    skew_part = pair_gram * spread / denom
    unit_matrix = jnp.eye(size_n, dtype=pair_gram.dtype)
    minus_part = unit_matrix - skew_part
    system = unit_matrix - jnp.dot(skew_part, skew_part, precision=lax.Precision.HIGHEST)
    product = jnp.dot(minus_part, minus_part, precision=lax.Precision.HIGHEST)
    factor = jnp.linalg.cholesky(system)
    return jax.scipy.linalg.cho_solve((factor, True), product.T).T


def square_sums(rows_part):
    row_ids = jnp.arange(rows_part.shape[1], dtype=jnp.int32)[:, None]
    col_ids = jnp.arange(rows_part.shape[2], dtype=jnp.int32)[None, :]
    on_diag = (row_ids == col_ids)[None, :, :]
    squares = rows_part * rows_part
    return (jnp.sum(jnp.where(on_diag, 0.0, squares)), jnp.sum(jnp.where(on_diag, squares, 0.0)))


def on_device(r_factor, block_slots):
    rows_in, total_cols = r_factor.shape
    blocks = total_cols // BLOCK
    pair_width = 2 * BLOCK
    arranged = jnp.take(r_factor.reshape(rows_in, blocks, BLOCK), block_slots, axis=1)
    arranged = arranged.reshape(rows_in, blocks // 2, pair_width)
    received = lax.all_to_all(arranged, "pair", split_axis=1, concat_axis=0, tiled=True)
    column = jnp.transpose(received, (1, 0, 2))
    local_pairs = column.shape[0]
    rows_here = column.shape[1]
    totals = None
    for sweep in range(ITERS):
        partial_value = jnp.einsum("pri,prj->pij", column, column, precision=lax.Precision.HIGHEST)
        pair_gram = lax.psum(partial_value, "row")
        if sweep == 0:
            off_part, diag_part = square_sums(pair_gram)
            totals = lax.psum((off_part, diag_part), "pair")
        rotation = jax.vmap(cayley)(pair_gram)
        column = jnp.einsum("pri,pij->prj", column, rotation, precision=lax.Precision.HIGHEST)
    upper_half = column[:, :, :BLOCK]
    lower_half = column[:, :, BLOCK:]
    pair_index = lax.axis_index("pair")
    pair_count = lax.axis_size("pair")
    global_ids = pair_index * local_pairs + jnp.arange(local_pairs, dtype=jnp.int32)
    last_id = pair_count * local_pairs - 1
    first_mask = (global_ids == 0)[:, None, None]
    last_mask = (global_ids == last_id)[:, None, None]
    forward = jnp.where(first_mask, lower_half, upper_half)
    came_up = passed_along(forward[local_pairs - 1], "pair", 1)
    came_down = passed_along(lower_half[0], "pair", -1)
    before = jnp.concatenate([came_up[None], forward[: local_pairs - 1]], axis=0)
    after = jnp.concatenate([lower_half[1:], came_down[None]], axis=0)
    new_upper = jnp.where(first_mask, upper_half, before)
    new_lower = jnp.where(last_mask, upper_half, after)
    joined = jnp.concatenate([new_upper, new_lower], axis=2)
    rotated = jnp.transpose(joined, (1, 0, 2)).reshape(rows_here, local_pairs * pair_width)
    off_ratio = jnp.sqrt(totals[0] / totals[1])
    return (rotated, off_ratio)


def solution(mesh):
    in_specs = (P(("row", "pair"), None), P())
    out_specs = (P("row", "pair"), P())
    return jax.shard_map(
        on_device, mesh=mesh, in_specs=in_specs, out_specs=out_specs, check_vma=False
    )
```

profile of v0, /device:TPU:32, one launch (start us, length us, event | category | flops | bytes accessed | tf_op | source)
XLA Modules:
  0.0 870.0 jit_solution(1644041194459896223)
XLA Ops:
  7.2 0.7 compare_and_fusion
  7.9 0.7 compare_select_fusion
  8.5 0.2 broadcast_in_dim.98
  8.9 4.3 reshape.87
  13.2 6.5 copy.172
  19.7 5.0 gather_fusion
  24.7 6.5 copy.173
  31.3 3.3 gather.17
  34.5 0.2 broadcast_select_fusion
  34.7 2.5 copy.174
  37.3 9.8 %all-to-all-start = ((f32[32,128,128]{2,0,1:T(8,128)}), f32[32,128,128]{2,0,1:T(8,128)S(1)}, u32[]{:S(2)}, u32[]{:S(2)}) async-start(f32[32,128,128]{2,0,1:T(8,128)} %copy.174), calls=%async_computation | async-start | bytes 4194304 | tf_op jit(solution)/shard_map/all_to_all | solution.py:44
  47.1 0.3 all-reduce.5.cloned.1.call-start
  47.4 46.9 %all-to-all-done = f32[32,128,128]{2,0,1:T(8,128)S(1)} async-done(((f32[32,128,128]{2,0,1:T(8,128)}), f32[32,128,128]{2,0,1:T(8,128)S(1)}, u32[]{:S(2)}, u32[]{:S(2)}) %all-to-all-start) | async-done | bytes 2097184 | tf_op jit(solution)/shard_map/all_to_all | solution.py:44
  94.3 1.3 copy-done.3
  95.6 1.8 copy.175
  97.4 4.3 fusion.33
  101.8 119.5 %all-reduce.5.cloned.1.call-done = f32[4,128,128]{1,2,0:T(8,128)} async-done(((f32[4,128,128]{1,2,0:T(8,128)}), f32[4,128,128]{1,2,0:T(8,128)}) %all-reduce.5.cloned.1.call-update) | async-done | bytes 262160 | tf_op jit(solution)/shard_map/psum | solution.py:51
  221.3 8.5 copy.178
  229.7 1.8 gather_fusion.1
  231.6 0.7 convolution_subtract_fusion.2
  232.3 0.1 copy.183
  232.4 46.9 %custom-call.18 = f32[4,128,128]{2,1,0:T(8,128)S(1)} custom-call(f32[4,128,128]{2,1,0:T(8,128)S(1)} %fusion.14), custom_call_target="Cholesky" | custom-call | tf_op jit(solution)/shard_map/vmap(jit(cholesky))/cholesky | solution.py:26
  279.6 39.7 %custom-call.19 = f32[4,1,128,128]{2,3,1,0:T(8,128)S(1)} custom-call(f32[4,1,128,128]{3,2,1,0:T(8,128)S(1)} %select_bitcast_fusion.2), custom_call_target="InvertDiagBlocksLowerTriangular" | custom-call | tf_op jit(solution)/shard_map/vmap(jit(_cho_solve))/triangular_solve | solution.py:27
  319.3 0.6 fusion.19
  320.0 0.6 fusion.12
  320.6 0.4 fusion.10
  321.0 1.9 fusion.34
  323.0 1.3 copy-done
  324.3 4.3 fusion.35
  328.6 116.2 %all-reduce.7.cloned.1.call-done = f32[4,128,128]{1,2,0:T(8,128)} async-done(((f32[4,128,128]{1,2,0:T(8,128)}), f32[4,128,128]{1,2,0:T(8,128)}) %all-reduce.7.cloned.1.call-update) | async-done | bytes 262160 | tf_op jit(solution)/shard_map/psum | solution.py:51
  444.8 8.5 copy.188
  453.3 1.8 gather_fusion.2
  455.2 0.7 convolution_subtract_fusion.1
  455.9 0.1 copy.193
  456.0 46.9 %custom-call.20 = f32[4,128,128]{2,1,0:T(8,128)S(1)} custom-call(f32[4,128,128]{2,1,0:T(8,128)S(1)} %fusion.9), custom_call_target="Cholesky" | custom-call | tf_op jit(solution)/shard_map/vmap(jit(cholesky))/cholesky | solution.py:26
  503.2 39.5 %custom-call.21 = f32[4,1,128,128]{2,3,1,0:T(8,128)S(1)} custom-call(f32[4,1,128,128]{3,2,1,0:T(8,128)S(1)} %select_bitcast_fusion.1), custom_call_target="InvertDiagBlocksLowerTriangular" | custom-call | tf_op jit(solution)/shard_map/vmap(jit(_cho_solve))/triangular_solve | solution.py:27
  542.7 0.6 fusion.17
  543.4 0.6 fusion.7
  544.0 0.4 fusion.5
  544.4 3.5 fusion.36
  547.9 4.3 fusion.37
  552.2 116.0 %all-reduce.9.cloned.1.call-done = f32[4,128,128]{1,2,0:T(8,128)} async-done(((f32[4,128,128]{1,2,0:T(8,128)}), f32[4,128,128]{1,2,0:T(8,128)}) %all-reduce.9.cloned.1.call-update) | async-done | bytes 262160 | tf_op jit(solution)/shard_map/psum | solution.py:51
  668.3 8.5 copy.198
  676.7 1.8 gather_fusion.3
  678.6 0.7 convolution_subtract_fusion
  679.2 0.1 copy.203
  679.4 0.7 fusion.4
  680.1 47.9 %custom-call.22 = f32[4,128,128]{2,1,0:T(8,128)S(1)} custom-call(f32[4,128,128]{2,1,0:T(8,128)} %fusion.4), custom_call_target="Cholesky" | custom-call | tf_op jit(solution)/shard_map/vmap(jit(cholesky))/cholesky | solution.py:26
  728.3 39.3 %custom-call.23 = f32[4,1,128,128]{2,3,1,0:T(8,128)S(1)} custom-call(f32[4,1,128,128]{3,2,1,0:T(8,128)S(1)} %select_bitcast_fusion), custom_call_target="InvertDiagBlocksLowerTriangular" | custom-call | tf_op jit(solution)/shard_map/vmap(jit(_cho_solve))/triangular_solve | solution.py:27
  767.6 0.7 fusion.15
  768.3 0.6 fusion.2
  768.9 0.4 fusion
  769.3 2.0 fusion.38
  771.3 0.8 slice_bitcast_fusion
  772.1 4.6 collective-permute-start.1
  776.7 0.2 slice_select_fusion
  776.9 0.7 slice_bitcast_fusion.1
  777.6 1.9 collective-permute-start
  779.6 0.8 select_reduce_fusion.3
  780.4 75.6 %all-reduce = (f32[]{:T(128)}, f32[]{:T(128)}) all-reduce(f32[]{:T(128)} %get-tuple-element.15, f32[]{:T(128)} %get-tuple-element.14), channel_id=1, replica_groups=mesh['pair'=32,'row'=16] {'pair'}, use_global_device_ids=true, to_apply=%region_6.9 | all-reduce | flops 2 | bytes 16 | tf_op jit(solution)/shard_map/psum | solution.py:54
  857.2 1.2 slice.50
  858.5 1.4 maximum_select_fusion
  860.0 0.1 pad_maximum_fusion
  860.1 1.8 copy.206
  (48 shorter events, 1.6 us)
Async XLA Ops:
  37.3 57.0 %all-to-all-start = ((f32[32,128,128]{2,0,1:T(8,128)}), f32[32,128,128]{2,0,1:T(8,128)S(1)}, u32[]{:S(2)}, u32[]{:S(2)}) async-start(f32[32,128,128]{2,0,1:T(8,128)} %copy.174), calls=%async_computation | async-start | bytes 4194304 | tf_op jit(solution)/shard_map/all_to_all | solution.py:44
  47.1 174.2 %all-reduce.5.cloned.1.call-start = ((), (), s32[]{:S(2)}) async-start(), calls=%async_computation.1 | async-start | bytes 524288 | tf_op jit(solution)/shard_map/psum | solution.py:51
  94.3 1.3 copy-start.3
  101.7 343.1 %all-reduce.7.cloned.1.call-start = ((), (), s32[]{:S(2)}) async-start(), calls=%async_computation.2 | async-start | bytes 524288 | tf_op jit(solution)/shard_map/psum | solution.py:51
  221.3 10.3 %copy-start.4 = (f32[4,128,128]{1,2,0:T(8,128)S(1)}, f32[4,128,128]{1,2,0:T(8,128)}, u32[]{:S(2)}) copy-start(f32[4,128,128]{1,2,0:T(8,128)} %all-reduce.5.cloned.1.call-done) | copy-start | bytes 786436
  323.0 1.3 copy-start
  328.6 339.7 %all-reduce.9.cloned.1.call-start = ((), (), s32[]{:S(2)}) async-start(), calls=%async_computation.3 | async-start | bytes 524288 | tf_op jit(solution)/shard_map/psum | solution.py:51
  444.8 10.4 %copy-start.6 = (f32[4,128,128]{1,2,0:T(8,128)S(1)}, f32[4,128,128]{1,2,0:T(8,128)}, u32[]{:S(2)}) copy-start(f32[4,128,128]{1,2,0:T(8,128)} %all-reduce.7.cloned.1.call-done) | copy-start | bytes 786436
  668.3 10.3 %copy-start.5 = (f32[4,128,128]{1,2,0:T(8,128)S(1)}, f32[4,128,128]{1,2,0:T(8,128)}, u32[]{:S(2)}) copy-start(f32[4,128,128]{1,2,0:T(8,128)} %all-reduce.9.cloned.1.call-done) | copy-start | bytes 786436
  771.3 6.3 copy-start.1
  772.1 86.4 %collective-permute-start.1 = (f32[1024,64]{0,1:T(8,128)}, f32[1024,64]{0,1:T(8,128)}, u32[]{:S(2)}, u32[]{:S(2)}) collective-permute-start(f32[1024,64]{0,1:T(8,128)} %slice_bitcast_fusion), channel_id=1, source_target_pairs={{16,0},{32,16},{48,32},{64,48},{80,64},{96,80},{112,96},{128,112},... | collective-permute-start | bytes 786440 | tf_op jit(solution)/shard_map/ppermute | solution.py:13
  777.6 80.9 %collective-permute-start = (f32[1024,64]{0,1:T(8,128)}, f32[1024,64]{0,1:T(8,128)}, u32[]{:S(2)}, u32[]{:S(2)}) collective-permute-start(f32[1024,64]{0,1:T(8,128)} %slice_bitcast_fusion.1), channel_id=1, source_target_pairs={{0,16},{16,32},{32,48},{48,64},{64,80},{80,96},{96,112},{112,128},... | collective-permute-start | bytes 786440 | tf_op jit(solution)/shard_map/ppermute | solution.py:13
  779.5 79.0 %copy-start.2 = (f32[4,1024,128]{1,2,0:T(8,128)S(1)}, f32[4,1024,128]{1,2,0:T(8,128)}, u32[]{:S(2)}) copy-start(f32[4,1024,128]{1,2,0:T(8,128)} %copy-done.1) | copy-start | bytes 6291460
Sparse Core Ops, SparseCore 0:
  101.8 119.4 all-reduce.4
  328.7 116.0 all-reduce.6
  552.3 115.8 all-reduce.8
where the time goes:
time: 877 us; the launch traced here: 870 us
  waiting for transfers between devices  399 us (45%)
  other arithmetic  266 us (30%)
  blocking collectives  75.6 us (9%)
  local copies, waits for them, and re-layouts  68.9 us (8%)
  matrix products  27.1 us (3%)
  between operations  17 us (2%)
  starting transfers between devices  16.6 us (2%)
    psum x3, waiting for transfers between devices, on_device(): pair_gram = lax.psum(partial_value, 'row')  352 us
    another operation x10, other arithmetic, cayley(): factor = jnp.linalg.cholesky(system)  142 us
    another operation x7, other arithmetic, cayley(): return jax.scipy.linalg.cho_solve((factor, True), product.T).T  119 us
    psum x1, blocking collectives, on_device(): totals = lax.psum((off_part, diag_part), 'pair')  75.6 us
    all_to_all x1, waiting for transfers between devices, on_device(): lax.all_to_all(arranged, 'pair', split_axis=1, concat_axis=0, tiled=True)  46.9 us
    psum x3, local copies, waits for them, and re-layouts, on_device(): pair_gram = lax.psum(partial_value, 'row')  25.4 us
  transfers between devices with their start and end apart: 6, of which 4 were waited for; matrix products, arithmetic and copies ran while one was open for 0% of the time, Pallas kernels for 0%

commit v1 on v0

--- a/solution.py
+++ b/solution.py
@@ -41,7 +41,10 @@
     pair_width = 2 * BLOCK
     arranged = jnp.take(r_factor.reshape(rows_in, blocks, BLOCK), block_slots, axis=1)
     arranged = arranged.reshape(rows_in, blocks // 2, pair_width)
-    received = lax.all_to_all(arranged, "pair", split_axis=1, concat_axis=0, tiled=True)
+    peers = lax.axis_size("pair")
+    tiles = jnp.stack(jnp.split(arranged, peers, axis=1), axis=0)
+    tiles = lax.all_to_all(tiles, "pair", split_axis=0, concat_axis=0)
+    received = jnp.concatenate(tiles, axis=0)
     column = jnp.transpose(received, (1, 0, 2))
     local_pairs = column.shape[0]
     rows_here = column.shape[1]

time: 877 us -> 894 us (1.019)
  local copies, waits for them, and re-layouts: 68.9 us -> 85.8 us
    unnamed x15 -> x44, local copies, waits for them, and re-layouts: 4.47 us -> 23.2 us
where the time goes in v1:
time: 894 us; the launch traced here: 887 us
  waiting for transfers between devices  399 us (45%)
  other arithmetic  266 us (30%)
  local copies, waits for them, and re-layouts  85.8 us (10%)
  blocking collectives  72.6 us (8%)
  matrix products  27.1 us (3%)
  starting transfers between devices  19.5 us (2%)
  between operations  17.1 us (2%)
    psum x3, waiting for transfers between devices, on_device(): pair_gram = lax.psum(partial_value, 'row')  352 us
    another operation x10, other arithmetic, cayley(): factor = jnp.linalg.cholesky(system)  142 us
    another operation x7, other arithmetic, cayley(): return jax.scipy.linalg.cho_solve((factor, True), product.T).T  119 us
    psum x1, blocking collectives, on_device(): totals = lax.psum((off_part, diag_part), 'pair')  72.6 us
    all_to_all x1, waiting for transfers between devices, on_device(): tiles = lax.all_to_all(tiles, 'pair', split_axis=0, concat_axis=0)  46.9 us
    psum x3, local copies, waits for them, and re-layouts, on_device(): pair_gram = lax.psum(partial_value, 'row')  25.4 us
    unnamed x44, local copies, waits for them, and re-layouts  23.2 us
  transfers between devices with their start and end apart: 6, of which 4 were waited for; matrix products, arithmetic and copies ran while one was open for 0% of the time, Pallas kernels for 0%

profile of v1, /device:TPU:32, one launch (start us, length us, event | category | flops | bytes accessed | tf_op | source)
XLA Modules:
  0.0 886.8 jit_solution(4957659918106718826)
XLA Ops:
  7.2 0.7 compare_select_fusion
  7.8 0.7 compare_and_fusion
  8.5 4.3 reshape.90
  12.8 6.5 copy.155
  19.3 5.0 gather_fusion
  24.3 6.5 copy.156
  30.9 3.3 gather.17
  34.7 0.6 fusion.55
  35.4 0.6 fusion.54
  36.7 0.6 fusion.52
  38.0 0.6 fusion.50
  39.3 0.6 fusion.48
  40.6 0.6 fusion.46
  41.9 0.6 fusion.44
  43.2 0.6 fusion.42
  44.5 0.6 fusion.40
  45.8 0.6 fusion.38
  47.0 0.6 fusion.36
  48.3 0.6 fusion.34
  49.6 0.6 fusion.32
  50.9 0.6 fusion.30
  52.2 0.6 fusion.28
  53.5 0.6 fusion.26
  54.8 0.6 fusion.24
  55.5 9.9 %all-to-all-start = ((f32[32,32,4,128]{3,2,1,0:T(4,128)}), f32[32,32,4,128]{3,2,1,0:T(4,128)}, u32[]{:S(2)}, u32[]{:S(2)}) async-start(f32[32,32,4,128]{3,2,1,0:T(4,128)} %fusion.24), calls=%async_computation | async-start | bytes 4194304 | tf_op jit(solution)/shard_map/all_to_all | solution.py:46
  65.7 46.9 %all-to-all-done = f32[32,32,4,128]{3,2,1,0:T(4,128)} async-done(((f32[32,32,4,128]{3,2,1,0:T(4,128)}), f32[32,32,4,128]{3,2,1,0:T(4,128)}, u32[]{:S(2)}, u32[]{:S(2)}) %all-to-all-start) | async-done | bytes 2097184 | tf_op jit(solution)/shard_map/all_to_all | solution.py:46
  112.6 1.9 copy.157
  114.5 4.3 fusion.65
  118.8 119.6 %all-reduce.5.cloned.1.call-done = f32[4,128,128]{1,2,0:T(8,128)} async-done(((f32[4,128,128]{1,2,0:T(8,128)}), f32[4,128,128]{1,2,0:T(8,128)}) %all-reduce.5.cloned.1.call-update) | async-done | bytes 262160 | tf_op jit(solution)/shard_map/psum | solution.py:54
  238.5 8.5 copy.160
  246.9 1.8 gather_fusion.1
  248.8 0.7 convolution_subtract_fusion.2
  249.6 46.9 %custom-call.18 = f32[4,128,128]{2,1,0:T(8,128)S(1)} custom-call(f32[4,128,128]{2,1,0:T(8,128)S(1)} %fusion.14), custom_call_target="Cholesky" | custom-call | tf_op jit(solution)/shard_map/vmap(jit(cholesky))/cholesky | solution.py:26
  296.8 39.7 %custom-call.19 = f32[4,1,128,128]{2,3,1,0:T(8,128)S(1)} custom-call(f32[4,1,128,128]{3,2,1,0:T(8,128)S(1)} %select_bitcast_fusion.2), custom_call_target="InvertDiagBlocksLowerTriangular" | custom-call | tf_op jit(solution)/shard_map/vmap(jit(_cho_solve))/triangular_solve | solution.py:27
  336.5 0.6 fusion.19
  338.2 1.9 fusion.66
  340.2 1.3 copy-done
  341.5 4.3 fusion.67
  345.8 116.0 %all-reduce.7.cloned.1.call-done = f32[4,128,128]{1,2,0:T(8,128)} async-done(((f32[4,128,128]{1,2,0:T(8,128)}), f32[4,128,128]{1,2,0:T(8,128)}) %all-reduce.7.cloned.1.call-update) | async-done | bytes 262160 | tf_op jit(solution)/shard_map/psum | solution.py:54
  461.8 8.5 copy.170
  470.3 1.8 gather_fusion.2
  472.2 0.7 convolution_subtract_fusion.1
  473.0 46.9 %custom-call.20 = f32[4,128,128]{2,1,0:T(8,128)S(1)} custom-call(f32[4,128,128]{2,1,0:T(8,128)S(1)} %fusion.9), custom_call_target="Cholesky" | custom-call | tf_op jit(solution)/shard_map/vmap(jit(cholesky))/cholesky | solution.py:26
  520.2 39.5 %custom-call.21 = f32[4,1,128,128]{2,3,1,0:T(8,128)S(1)} custom-call(f32[4,1,128,128]{3,2,1,0:T(8,128)S(1)} %select_bitcast_fusion.1), custom_call_target="InvertDiagBlocksLowerTriangular" | custom-call | tf_op jit(solution)/shard_map/vmap(jit(_cho_solve))/triangular_solve | solution.py:27
  561.4 3.5 fusion.68
  564.9 4.3 fusion.69
  569.2 116.1 %all-reduce.9.cloned.1.call-done = f32[4,128,128]{1,2,0:T(8,128)} async-done(((f32[4,128,128]{1,2,0:T(8,128)}), f32[4,128,128]{1,2,0:T(8,128)}) %all-reduce.9.cloned.1.call-update) | async-done | bytes 262160 | tf_op jit(solution)/shard_map/psum | solution.py:54
  685.3 8.5 copy.180
  693.8 1.8 gather_fusion.3
  695.6 0.7 convolution_subtract_fusion
  696.4 0.7 fusion.4
  697.1 47.9 %custom-call.22 = f32[4,128,128]{2,1,0:T(8,128)S(1)} custom-call(f32[4,128,128]{2,1,0:T(8,128)} %fusion.4), custom_call_target="Cholesky" | custom-call | tf_op jit(solution)/shard_map/vmap(jit(cholesky))/cholesky | solution.py:26
  745.3 39.3 %custom-call.23 = f32[4,1,128,128]{2,3,1,0:T(8,128)S(1)} custom-call(f32[4,1,128,128]{3,2,1,0:T(8,128)S(1)} %select_bitcast_fusion), custom_call_target="InvertDiagBlocksLowerTriangular" | custom-call | tf_op jit(solution)/shard_map/vmap(jit(_cho_solve))/triangular_solve | solution.py:27
  784.7 0.7 fusion.15
  786.3 2.0 fusion.70
  788.3 0.8 slice_bitcast_fusion
  789.4 0.7 slice_bitcast_fusion.1
  790.1 3.4 collective-permute-start
  793.5 5.9 collective-permute-start.1
  799.4 0.8 select_reduce_fusion.3
  800.2 72.6 %all-reduce = (f32[]{:T(128)}, f32[]{:T(128)}) all-reduce(f32[]{:T(128)} %get-tuple-element.13, f32[]{:T(128)} %get-tuple-element.12), channel_id=1, replica_groups=mesh['pair'=32,'row'=16] {'pair'}, use_global_device_ids=true, to_apply=%region_6.9 | all-reduce | flops 2 | bytes 16 | tf_op jit(solution)/shard_map/psum | solution.py:57
  874.1 1.2 slice.50
  875.3 1.4 maximum_select_fusion
  876.9 1.8 copy.188
  (77 shorter events, 16.3 us)
Async XLA Ops:
  55.5 57.1 %all-to-all-start = ((f32[32,32,4,128]{3,2,1,0:T(4,128)}), f32[32,32,4,128]{3,2,1,0:T(4,128)}, u32[]{:S(2)}, u32[]{:S(2)}) async-start(f32[32,32,4,128]{3,2,1,0:T(4,128)} %fusion.24), calls=%async_computation | async-start | bytes 4194304 | tf_op jit(solution)/shard_map/all_to_all | solution.py:46
  65.4 173.1 %all-reduce.5.cloned.1.call-start = ((), (), s32[]{:S(2)}) async-start(), calls=%async_computation.1 | async-start | bytes 524288 | tf_op jit(solution)/shard_map/psum | solution.py:54
  118.8 343.0 %all-reduce.7.cloned.1.call-start = ((), (), s32[]{:S(2)}) async-start(), calls=%async_computation.2 | async-start | bytes 524288 | tf_op jit(solution)/shard_map/psum | solution.py:54
  238.5 10.3 %copy-start.3 = (f32[4,128,128]{1,2,0:T(8,128)S(1)}, f32[4,128,128]{1,2,0:T(8,128)}, u32[]{:S(2)}) copy-start(f32[4,128,128]{1,2,0:T(8,128)} %all-reduce.5.cloned.1.call-done) | copy-start | bytes 786436
  340.1 1.3 copy-start
  345.8 339.5 %all-reduce.9.cloned.1.call-start = ((), (), s32[]{:S(2)}) async-start(), calls=%async_computation.3 | async-start | bytes 524288 | tf_op jit(solution)/shard_map/psum | solution.py:54
  461.8 10.4 %copy-start.5 = (f32[4,128,128]{1,2,0:T(8,128)S(1)}, f32[4,128,128]{1,2,0:T(8,128)}, u32[]{:S(2)}) copy-start(f32[4,128,128]{1,2,0:T(8,128)} %all-reduce.7.cloned.1.call-done) | copy-start | bytes 786436
  685.3 10.3 %copy-start.4 = (f32[4,128,128]{1,2,0:T(8,128)S(1)}, f32[4,128,128]{1,2,0:T(8,128)}, u32[]{:S(2)}) copy-start(f32[4,128,128]{1,2,0:T(8,128)} %all-reduce.9.cloned.1.call-done) | copy-start | bytes 786436
  788.3 1.8 copy-start.1
  790.1 85.2 %collective-permute-start = (f32[1024,64]{0,1:T(8,128)}, f32[1024,64]{0,1:T(8,128)}, u32[]{:S(2)}, u32[]{:S(2)}) collective-permute-start(f32[1024,64]{0,1:T(8,128)} %slice_bitcast_fusion.1), channel_id=1, source_target_pairs={{0,16},{16,32},{32,48},{48,64},{64,80},{80,96},{96,112},{112,128},... | collective-permute-start | bytes 786440 | tf_op jit(solution)/shard_map/ppermute | solution.py:13
  793.5 81.9 %copy-start.2 = (f32[4,1024,128]{1,2,0:T(8,128)S(1)}, f32[4,1024,128]{1,2,0:T(8,128)}, u32[]{:S(2)}) copy-start(f32[4,1024,128]{1,2,0:T(8,128)} %copy-done.1) | copy-start | bytes 6291460
  793.5 81.9 %collective-permute-start.1 = (f32[1024,64]{0,1:T(8,128)}, f32[1024,64]{0,1:T(8,128)}, u32[]{:S(2)}, u32[]{:S(2)}) collective-permute-start(f32[1024,64]{0,1:T(8,128)} %slice_bitcast_fusion), channel_id=1, source_target_pairs={{16,0},{32,16},{48,32},{64,48},{80,64},{96,80},{112,96},{128,112},... | collective-permute-start | bytes 786440 | tf_op jit(solution)/shard_map/ppermute | solution.py:13
Sparse Core Ops, SparseCore 0:
  118.9 119.5 all-reduce.4
  345.9 115.8 all-reduce.6
  569.3 115.9 all-reduce.8
